TPU v7x, 32 devices: a whole 2x2x4 slice. The times are simulated.
32 devices in a mesh: groups: 2 (over x), row: 16 (over z, y, core).
Axes of the slice: x: 2, y: 2, z: 4, core: 2. Of those that a mesh axis runs over, the one named last changes fastest.
Arguments:
- atom_feat: bfloat16 [8192, 128], P(('groups', 'row')), parts along dimension 0, may hold values from -8 to 8
- window_start: int32 [256], P(('groups', 'row')), parts along dimension 0, may hold values from -64 to 4032, as said below
- atom_count: int32 [512], P(('groups', 'row')), parts along dimension 0, may hold values from 1 to 24, as said below
- residue_type: int32 [512], P(('groups', 'row')), parts along dimension 0, may hold values from 0 to 31
- chain_id: int32 [512], P(('groups', 'row')), parts along dimension 0, may hold values from 0 to 5, never falling along the last dimension, each value on 1 to 64 neighbouring positions
- token_single: bfloat16 [512, 768], P(('groups', 'row')), parts along dimension 0, may hold values from -6 to 6
- pair: bfloat16 [512, 256, 128], P(('groups', 'row')), parts along dimension 0, may hold values from -8 to 8
- atom_gain: float32 [128], replicated, may hold values from 0.25 to 1.75
- atom_qkv: bfloat16 [128, 384], replicated, may hold values from -1 to 1
- atom_out: bfloat16 [128, 128], replicated, may hold values from -0.5 to 0.5
- pool_weight: bfloat16 [128, 768], replicated, may hold values from -0.5 to 0.5
- restype_table: bfloat16 [32, 768], replicated, may hold values from -3 to 3
- token_gain: float32 [768], replicated, may hold values from 0.25 to 1.75
- token_proj: bfloat16 [768, 3072], replicated, may hold values from -0.21875 to 0.21875
- token_out: bfloat16 [768, 768], replicated, may hold values from -0.21875 to 0.21875
- pair_gain: float32 [128], replicated, may hold values from 0.1 to 1.9
- pair_bias_weight: bfloat16 [128, 16], replicated, may hold values from -16 to 16
- chain_weight: float32 [16], replicated, may hold values from -2 to 2
- back_weight: bfloat16 [768, 128], replicated, may hold values from -0.21875 to 0.21875
Outputs:
- atoms_out: bfloat16 [8192, 128], P(('groups', 'row')), parts along dimension 0
- tokens_out: bfloat16 [512, 768], P(('groups', 'row')), parts along dimension 0
There are 2 independent parts, one for each index of `groups`. A program takes and returns all parts, laid end to end along the dimension named above; an argument that names none is the same for every part. Nothing has to cross between parts.
Inputs may be any that keep to these rules, and one draw needn't show every extreme that they name: `window_start`: key window b begins within 16 of b * 32 + 32 // 2 - 128 // 2. `atom_count`: atoms of token t follow those of token t - 1 and the counts sum to 4096; for every k, the first atom of token k * 16 lies within 64 of atom k * 256. `chain_id`: chain numbers never fall along the tokens.
All inputs are finite; a program needn't handle non-finite values.
Results may differ from a plain program's by a relative error of at most 0.008.
Values may be sent and summed in bfloat16 or wider, within the bound.
A program may use at most 64 MiB of HBM per device.

v0:
```python
import math

import jax
import jax.numpy as jnp
from jax import lax
from jax.sharding import PartitionSpec as P

CA = 128
CS = 768
HEADS = 16
AHEADS = 4
RESTYPES = 32
QBLK = 32
KWIN = 128
HDIM = 48
ADIM = 32
HALO = 64


def extended(x, sides, width):
    for axis, dim in sides:
        size, length = (lax.axis_size(axis), x.shape[dim])
        up = [(i, (i + 1) % size) for i in range(size - 1)]
        down = [(j, i) for i, j in up]
        last = lax.slice_in_dim(x, length - width, length, axis=dim)
        initial = lax.slice_in_dim(x, 0, width, axis=dim)
        before = lax.ppermute(last, axis, up)
        after = lax.ppermute(initial, axis, down)
        x = jnp.concatenate([before, x, after], axis=dim)
    return x


def layer_norm(values, gain):
    centered = values - jnp.mean(values, axis=-1, keepdims=True)
    variance = jnp.mean(centered * centered, axis=-1, keepdims=True)
    return centered * lax.rsqrt(variance + 1e-05) * gain


def window_attend(queries, windows, inside):
    blocks = queries.shape[0]
    keys = windows[:, :, :CA].reshape(blocks, KWIN, AHEADS, ADIM)
    values = windows[:, :, CA:].reshape(blocks, KWIN, AHEADS, ADIM)
    scores = jnp.einsum(
        "bqhd,bkhd->bhqk", queries, keys, preferred_element_type=jnp.float32
    ) / math.sqrt(ADIM)
    scores = jnp.where(inside[:, None, None, :], scores, -1000000000.0)
    weights = jnp.exp(scores - jnp.max(scores, axis=-1, keepdims=True))
    denom = jnp.sum(weights, axis=-1, keepdims=True)
    mixed = jnp.einsum(
        "bhqk,bkhd->bqhd", weights.astype(jnp.bfloat16), values, preferred_element_type=jnp.float32
    )
    mixed = mixed / jnp.transpose(denom, (0, 2, 1, 3))
    return mixed.reshape(blocks * QBLK, CA).astype(jnp.bfloat16)


def shards(
    atom_feat,
    window_start,
    atom_count,
    residue_type,
    chain_id,
    token_single,
    pair,
    atom_gain,
    atom_qkv,
    atom_out,
    pool_weight,
    restype_table,
    token_gain,
    token_proj,
    token_out,
    pair_gain,
    pair_bias_weight,
    chain_weight,
    back_weight,
):
    atom_rows = atom_feat.shape[0]
    token_rows = token_single.shape[0]
    device = lax.axis_index("row")
    all_atoms = atom_rows * lax.axis_size("row")
    counts_all = lax.all_gather(atom_count, "row", axis=0, tiled=True)
    ends = jnp.cumsum(counts_all)
    first_atom = device * atom_rows
    own_tokens = jnp.searchsorted(
        ends, first_atom + jnp.arange(atom_rows, dtype=jnp.int32), side="right"
    )
    nearby = (device - 1) * token_rows + jnp.arange(3 * token_rows, dtype=jnp.int32)
    normed = layer_norm(atom_feat.astype(jnp.float32), atom_gain).astype(jnp.bfloat16)
    atom_proj = jnp.dot(normed, atom_qkv, preferred_element_type=jnp.float32).astype(jnp.bfloat16)
    queries = atom_proj[:, :CA].reshape(atom_rows // QBLK, QBLK, AHEADS, ADIM)
    padded = extended(atom_proj[:, CA:], (("row", 0),), HALO)
    anchors = window_start - first_atom + HALO
    windows = jax.vmap(lambda anchor: lax.dynamic_slice_in_dim(padded, anchor, KWIN, 0))(anchors)
    position = window_start[:, None] + jnp.arange(KWIN, dtype=jnp.int32)[None, :]
    inside = (position >= 0) & (position < all_atoms)
    attended = window_attend(queries, windows, inside)
    atoms_mid = (
        atom_feat.astype(jnp.float32)
        + jnp.dot(attended, atom_out, preferred_element_type=jnp.float32)
    ).astype(jnp.bfloat16)
    lifted = jax.nn.relu(
        jnp.dot(atoms_mid, pool_weight, preferred_element_type=jnp.float32)
    ).astype(jnp.bfloat16)
    select = (nearby[:, None] == own_tokens[None, :]).astype(jnp.bfloat16)
    partial_value = jnp.dot(select, lifted, preferred_element_type=jnp.float32)
    edges = extended(partial_value.astype(jnp.bfloat16), (("row", 0),), token_rows).astype(
        partial_value.dtype
    )
    pooled = edges[:token_rows] + edges[2 * token_rows : 3 * token_rows] + edges[4 * token_rows :]
    onehot = (residue_type[:, None] == jnp.arange(RESTYPES, dtype=jnp.int32)[None, :]).astype(
        jnp.bfloat16
    )
    state = token_single.astype(jnp.float32) + pooled / atom_count[:, None].astype(jnp.float32)
    state = state + jnp.dot(onehot, restype_table, preferred_element_type=jnp.float32)
    token_normed = layer_norm(state, token_gain).astype(jnp.bfloat16)
    token_all = jnp.dot(token_normed, token_proj, preferred_element_type=jnp.float32)
    query = token_all[:, :CS].astype(jnp.bfloat16).reshape(token_rows, HEADS, HDIM)
    gate = jax.nn.sigmoid(token_all[:, 3 * CS :])
    pair_normed = layer_norm(pair.astype(jnp.float32), pair_gain).astype(jnp.bfloat16)
    bias = jnp.einsum(
        "tkc,ch->thk", pair_normed, pair_bias_weight, preferred_element_type=jnp.float32
    )
    projected = jnp.dot(
        lax.all_gather(token_normed, "row", axis=0, tiled=True),
        token_proj[:, CS : 3 * CS],
        preferred_element_type=jnp.float32,
    ).astype(jnp.bfloat16)
    keys = projected[:, :CS]
    running_max = jnp.full((token_rows, HEADS), -1e30, jnp.float32)
    extent = keys.shape[0]
    keys_heads = keys.reshape(extent, HEADS, HDIM)
    values_heads = projected[:, CS:].reshape(extent, HEADS, HDIM)
    scores = jnp.einsum(
        "thd,khd->thk", query, keys_heads, preferred_element_type=jnp.float32
    ) / math.sqrt(HDIM)
    scores = scores + bias
    same = (
        chain_id[:, None] == lax.all_gather(chain_id, "row", axis=0, tiled=True)[None, :]
    ).astype(jnp.float32)
    scores = scores + chain_weight[None, :, None] * same[:, None, :]
    newest = jnp.maximum(running_max, jnp.max(scores, axis=-1))
    weights = jnp.exp(scores - newest[:, :, None])
    summed = jnp.sum(weights, axis=-1)
    product = jnp.einsum(
        "thk,khd->thd",
        weights.astype(jnp.bfloat16),
        values_heads,
        preferred_element_type=jnp.float32,
    )
    mixed = product / summed[:, :, None]
    gated = (mixed.reshape(token_rows, CS) * gate).astype(jnp.bfloat16)
    tokens_out = (state + jnp.dot(gated, token_out, preferred_element_type=jnp.float32)).astype(
        jnp.bfloat16
    )
    back = jnp.dot(tokens_out, back_weight, preferred_element_type=jnp.float32).astype(jnp.bfloat16)
    beside_all = extended(back, (("row", 0),), token_rows)
    select_back = (own_tokens[:, None] == nearby[None, :]).astype(jnp.bfloat16)
    spread = jnp.dot(select_back, beside_all, preferred_element_type=jnp.float32)
    atoms_out = (atoms_mid.astype(jnp.float32) + spread).astype(jnp.bfloat16)
    return (atoms_out, tokens_out)


def solution(mesh):
    return jax.shard_map(
        shards,
        mesh=mesh,
        in_specs=(
            P(("groups", "row"), None),
            P(("groups", "row")),
            P(("groups", "row")),
            P(("groups", "row")),
            P(("groups", "row")),
            P(("groups", "row"), None),
            P(("groups", "row"), None, None),
            P(),
            P(),
            P(),
            P(),
            P(),
            P(),
            P(),
            P(),
            P(),
            P(),
            P(),
            P(),
        ),
        out_specs=(P(("groups", "row"), None), P(("groups", "row"), None)),
        check_vma=False,
    )
```

profile of v0, /device:TPU:5, one launch (start us, length us, event | category | flops | bytes accessed | tf_op | source)
XLA Modules:
  0.0 105.9 jit_solution(10534046000898941628)
XLA Ops:
  0.6 1.0 convert_reduce_fusion.1
  1.7 1.0 fusion.38
  2.7 1.2 %convolution_convert_fusion.1 = bf16[256,384]{1,0:T(8,128)(2,1)S(1)} fusion(bf16[128,384]{1,0:T(8,128)(2,1)} %param.29, bf16[256,128]{1,0:T(8,128)(2,1)} %param.21, f32[128]{0:T(128)} %param.28, f32[256]{0:T(256)S(1)} %add_rsqrt_fusion.1, f32[256]{0:T(256)S(1)} %broadcast_multiply_fusion.1), kind=kOutput, calls=%fused_computation.28 | convolution fusion | flops 25427968 | bytes 363008 | tf_op jit(solution)/shard_map/dot_general | solution.py:89
  4.0 3.7 %collective-permute-start = (bf16[64,256]{1,0:T(8,128)(2,1)S(1)}, bf16[64,256]{1,0:T(8,128)(2,1)S(1)}, u32[]{:S(2)}, u32[]{:S(2)}) collective-permute-start(bf16[64,256]{1,0:T(8,128)(2,1)S(1)} %get-tuple-element.123), channel_id=1, source_target_pairs={{0,1},{1,2},{2,3},{3,4},{4,5},{5,6},{6,7},{7,8},{8,9},{9,10},{10,1... | collective-permute-start | bytes 98312 | tf_op jit(solution)/shard_map/ppermute | solution.py:27
  7.7 1.9 %collective-permute-start.1 = (bf16[64,256]{1,0:T(8,128)(2,1)S(1)}, bf16[64,256]{1,0:T(8,128)(2,1)S(1)}, u32[]{:S(2)}, u32[]{:S(2)}) collective-permute-start(bf16[64,256]{1,0:T(8,128)(2,1)S(1)} %get-tuple-element.124), channel_id=1, source_target_pairs={{1,0},{2,1},{3,2},{4,3},{5,4},{6,5},{7,6},{8,7},{9,8},{10,9},{11,1... | collective-permute-start | bytes 98312 | tf_op jit(solution)/shard_map/ppermute | solution.py:28
  11.0 1.2 %dynamic-slice.4 = u32[1]{0:T(128)} dynamic-slice(u32[32]{0:T(128)} %constant.113, u32[]{:T(128)S(6)} %add.148), dynamic_slice_sizes={1} | dynamic-slice | bytes 12
  12.8 0.9 dynamic-update-slice.2
  13.7 0.8 dynamic-update-slice.3
  14.5 9.7 %all-reduce.3 = (s32[256]{0:T(256)S(1)}, s32[256]{0:T(256)S(1)}) all-reduce(s32[256]{0:T(256)S(1)} %dynamic-update-slice.2, s32[256]{0:T(256)S(1)} %dynamic-update-slice.3), channel_id=1, replica_groups=mesh['groups'=2,'row'=16] {'row'}, use_global_device_ids=true, to_apply=%add.1 | all-reduce | flops 512 | bytes 4096
  24.9 18.1 %while.26 = (s32[]{:T(128)}, u32[256]{0:T(256)S(1)}, u32[256]{0:T(256)S(1)}, s32[256]{0:T(256)S(1)}, s32[]{:T(128)}, /*index=5*/s32[]{:T(128)}, s32[]{:T(128)}, s32[]{}) while((s32[]{:T(128)}, u32[256]{0:T(256)S(1)}, u32[256]{0:T(256)S(1)}, s32[256]{0:T(256)S(1)}, s32[]{:T(128)}, /*index=5*/s32[]{:T(128)}, s32[]{:T(128)}, s32[]{}) %tuple.58), condition=%wide.region_7.8_spmd.clone, body=%wide.region_6.7_spmd.clone.sunk | while | flops 4612 | bytes 16496 | solution.py:84
  24.9 1.9 %gather_fusion = s32[256]{0:T(256)S(1)} fusion(s32[256]{0:T(256)S(1)} %get-tuple-element.227, u32[1024]{0:T(1024)S(1)} %pad_clamp_fusion.2), kind=kCustom, calls=%fused_computation.clone.clone.1 | custom fusion | bytes 3072 | tf_op jit(solution)/shard_map/jit(searchsorted)/jit(_searchsorted_scan_impl)/vmap(jit(_searchsorted_scan_impl))/while/body/eval_jaxpr/gather | solution.py:84
  26.9 1.9 %gather_fusion = s32[256]{0:T(256)S(1)} fusion(s32[256]{0:T(256)S(1)} %get-tuple-element.227, u32[1024]{0:T(1024)S(1)} %pad_clamp_fusion.2), kind=kCustom, calls=%fused_computation.clone.clone.1 | custom fusion | bytes 3072 | tf_op jit(solution)/shard_map/jit(searchsorted)/jit(_searchsorted_scan_impl)/vmap(jit(_searchsorted_scan_impl))/while/body/eval_jaxpr/gather | solution.py:84
  28.9 1.9 %gather_fusion = s32[256]{0:T(256)S(1)} fusion(s32[256]{0:T(256)S(1)} %get-tuple-element.227, u32[1024]{0:T(1024)S(1)} %pad_clamp_fusion.2), kind=kCustom, calls=%fused_computation.clone.clone.1 | custom fusion | bytes 3072 | tf_op jit(solution)/shard_map/jit(searchsorted)/jit(_searchsorted_scan_impl)/vmap(jit(_searchsorted_scan_impl))/while/body/eval_jaxpr/gather | solution.py:84
  30.9 1.9 %gather_fusion = s32[256]{0:T(256)S(1)} fusion(s32[256]{0:T(256)S(1)} %get-tuple-element.227, u32[1024]{0:T(1024)S(1)} %pad_clamp_fusion.2), kind=kCustom, calls=%fused_computation.clone.clone.1 | custom fusion | bytes 3072 | tf_op jit(solution)/shard_map/jit(searchsorted)/jit(_searchsorted_scan_impl)/vmap(jit(_searchsorted_scan_impl))/while/body/eval_jaxpr/gather | solution.py:84
  32.9 1.9 %gather_fusion = s32[256]{0:T(256)S(1)} fusion(s32[256]{0:T(256)S(1)} %get-tuple-element.227, u32[1024]{0:T(1024)S(1)} %pad_clamp_fusion.2), kind=kCustom, calls=%fused_computation.clone.clone.1 | custom fusion | bytes 3072 | tf_op jit(solution)/shard_map/jit(searchsorted)/jit(_searchsorted_scan_impl)/vmap(jit(_searchsorted_scan_impl))/while/body/eval_jaxpr/gather | solution.py:84
  34.9 1.9 %gather_fusion = s32[256]{0:T(256)S(1)} fusion(s32[256]{0:T(256)S(1)} %get-tuple-element.227, u32[1024]{0:T(1024)S(1)} %pad_clamp_fusion.2), kind=kCustom, calls=%fused_computation.clone.clone.1 | custom fusion | bytes 3072 | tf_op jit(solution)/shard_map/jit(searchsorted)/jit(_searchsorted_scan_impl)/vmap(jit(_searchsorted_scan_impl))/while/body/eval_jaxpr/gather | solution.py:84
  37.0 1.9 %gather_fusion = s32[256]{0:T(256)S(1)} fusion(s32[256]{0:T(256)S(1)} %get-tuple-element.227, u32[1024]{0:T(1024)S(1)} %pad_clamp_fusion.2), kind=kCustom, calls=%fused_computation.clone.clone.1 | custom fusion | bytes 3072 | tf_op jit(solution)/shard_map/jit(searchsorted)/jit(_searchsorted_scan_impl)/vmap(jit(_searchsorted_scan_impl))/while/body/eval_jaxpr/gather | solution.py:84
  39.0 1.9 %gather_fusion = s32[256]{0:T(256)S(1)} fusion(s32[256]{0:T(256)S(1)} %get-tuple-element.227, u32[1024]{0:T(1024)S(1)} %pad_clamp_fusion.2), kind=kCustom, calls=%fused_computation.clone.clone.1 | custom fusion | bytes 3072 | tf_op jit(solution)/shard_map/jit(searchsorted)/jit(_searchsorted_scan_impl)/vmap(jit(_searchsorted_scan_impl))/while/body/eval_jaxpr/gather | solution.py:84
  41.0 1.9 %gather_fusion = s32[256]{0:T(256)S(1)} fusion(s32[256]{0:T(256)S(1)} %get-tuple-element.227, u32[1024]{0:T(1024)S(1)} %pad_clamp_fusion.2), kind=kCustom, calls=%fused_computation.clone.clone.1 | custom fusion | bytes 3072 | tf_op jit(solution)/shard_map/jit(searchsorted)/jit(_searchsorted_scan_impl)/vmap(jit(_searchsorted_scan_impl))/while/body/eval_jaxpr/gather | solution.py:84
  43.4 1.3 %fusion.7 = f32[16,256]{1,0:T(8,128)S(1)} fusion(bf16[16,256,128]{2,1,0:T(8,128)(2,1)S(1)} %copy-done.1, f32[16,256]{1,0:T(8,128)S(1)} %broadcast_multiply_fusion), kind=kLoop, calls=%fused_computation.17 | loop fusion | flops 2093056 | bytes 1081344 | tf_op jit(solution)/shard_map/reduce_sum | solution.py:35
  44.7 2.6 %fusion.23 = f32[16,256,16]{1,2,0:T(8,128)S(1)} fusion(bf16[16,256,128]{2,1,0:T(8,128)(2,1)S(1)} %copy-done.1, f32[128]{0:T(128)S(1)} %copy-done.13, f32[16,256]{1,0:T(8,128)S(1)} %add_rsqrt_fusion, f32[16,256]{1,0:T(8,128)S(1)} %broadcast_multiply_fusion, bf16[128,16]{0,1:T(8,128)(2,1)S(1)} %copy-done.12), kind=kOutput, calls=%fused_computation.44 | convolution fusion | flops 19398656 | bytes 1348096 | tf_op jit(solution)/shard_map/tkc,ch->thk/dot_general | solution.py:120
  47.6 10.2 %while.25 = (s32[]{:T(128)}, bf16[384,256]{1,0:T(8,128)(2,1)S(1)}, s32[8,2]{0,1:T(2,128)S(1)}, bf16[8,128,256]{2,1,0:T(8,128)(2,1)S(1)}, s32[]{:T(128)}) while((s32[]{:T(128)}, bf16[384,256]{1,0:T(8,128)(2,1)S(1)}, s32[8,2]{0,1:T(2,128)S(1)}, bf16[8,128,256]{2,1,0:T(8,128)(2,1)S(1)}, s32[]{:T(128)}) %tuple.55), condition=%wide.while_cond, body=%wide.while_body.sunk | while | flops 2 | bytes 131169 | solution.py:93
  60.6 5.3 %collective-permute-start.2 = (bf16[16,768]{1,0:T(8,128)(2,1)S(1)}, bf16[16,768]{1,0:T(8,128)(2,1)S(1)}, u32[]{:S(2)}, u32[]{:S(2)}) collective-permute-start(bf16[16,768]{1,0:T(8,128)(2,1)S(1)} %get-tuple-element.125), channel_id=1, source_target_pairs={{0,1},{1,2},{2,3},{3,4},{4,5},{5,6},{6,7},{7,8},{8,9},{9,10},{10,1... | collective-permute-start | bytes 73736 | tf_op jit(solution)/shard_map/ppermute | solution.py:27
  65.9 1.9 %collective-permute-start.3 = (bf16[16,768]{1,0:T(8,128)(2,1)S(1)}, bf16[16,768]{1,0:T(8,128)(2,1)S(1)}, u32[]{:S(2)}, u32[]{:S(2)}) collective-permute-start(bf16[16,768]{1,0:T(8,128)(2,1)S(1)} %get-tuple-element.126), channel_id=1, source_target_pairs={{1,0},{2,1},{3,2},{4,3},{5,4},{6,5},{7,6},{8,7},{9,8},{10,9},{11,1... | collective-permute-start | bytes 73736 | tf_op jit(solution)/shard_map/ppermute | solution.py:28
  68.0 4.0 %collective-permute-done.3 = bf16[16,768]{1,0:T(8,128)(2,1)S(1)} collective-permute-done((bf16[16,768]{1,0:T(8,128)(2,1)S(1)}, bf16[16,768]{1,0:T(8,128)(2,1)S(1)}, u32[]{:S(2)}, u32[]{:S(2)}) %collective-permute-start.3) | collective-permute-done | bytes 24608 | tf_op jit(solution)/shard_map/ppermute | solution.py:28
  72.6 16.4 %all_gather.10 = bf16[256,768]{1,0:T(8,128)(2,1)S(1)} all-gather(bf16[16,768]{1,0:T(8,128)(2,1)S(1)} %multiply_convert_fusion), channel_id=1, replica_groups=mesh['groups'=2,'row'=16] {'row'}, dimensions={0}, use_global_device_ids=true | all-gather | bytes 417792 | tf_op jit(solution)/shard_map/all_gather | solution.py:124
  89.0 3.1 %fusion.85 = f32[16,3072]{1,0:T(8,128)S(1)} fusion(bf16[16,768]{1,0:T(8,128)(2,1)S(1)} %multiply_convert_fusion, bf16[768,3072]{1,0:T(8,128)(2,1)} %param.34), kind=kOutput, calls=%fused_computation.127 | convolution fusion | flops 75497472 | bytes 4939776 | tf_op jit(solution)/shard_map/dot_general | solution.py:116
  92.1 2.4 %convolution_convert_fusion = bf16[256,1536]{1,0:T(8,128)(2,1)S(1)} fusion(bf16[256,768]{1,0:T(8,128)(2,1)S(1)} %all_gather.10, bf16[768,3072]{1,0:T(8,128)(2,1)} %param.34), kind=kOutput, calls=%fused_computation.13 | convolution fusion | flops 604372992 | bytes 3538944 | tf_op jit(solution)/shard_map/dot_general | solution.py:123
  96.8 2.4 %collective-permute-start.4 = (bf16[16,128]{1,0:T(8,128)(2,1)S(1)}, bf16[16,128]{1,0:T(8,128)(2,1)S(1)}, u32[]{:S(2)}, u32[]{:S(2)}) collective-permute-start(bf16[16,128]{1,0:T(8,128)(2,1)S(1)} %convolution_convert_fusion.2), channel_id=1, source_target_pairs={{0,1},{1,2},{2,3},{3,4},{4,5},{5,6},{6,7},{7,8},{8,9},{9,10},{10,1... | collective-permute-start | bytes 12296 | tf_op jit(solution)/shard_map/ppermute | solution.py:27
  99.2 1.9 %collective-permute-start.5 = (bf16[16,128]{1,0:T(8,128)(2,1)S(1)}, bf16[16,128]{1,0:T(8,128)(2,1)S(1)}, u32[]{:S(2)}, u32[]{:S(2)}) collective-permute-start(bf16[16,128]{1,0:T(8,128)(2,1)S(1)} %convolution_convert_fusion.2), channel_id=1, source_target_pairs={{1,0},{2,1},{3,2},{4,3},{5,4},{6,5},{7,6},{8,7},{9,8},{10,9},{11,1... | collective-permute-start | bytes 12296 | tf_op jit(solution)/shard_map/ppermute | solution.py:28
  101.1 3.9 %collective-permute-done.5 = bf16[16,128]{1,0:T(8,128)(2,1)S(1)} collective-permute-done((bf16[16,128]{1,0:T(8,128)(2,1)S(1)}, bf16[16,128]{1,0:T(8,128)(2,1)S(1)}, u32[]{:S(2)}, u32[]{:S(2)}) %collective-permute-start.5) | collective-permute-done | bytes 4128 | tf_op jit(solution)/shard_map/ppermute | solution.py:28
  105.0 0.9 fusion.21
  (143 shorter events, 18.4 us)
Async XLA Ops:
  0.6 95.7 %copy-start = (bf16[768,768]{1,0:T(8,128)(2,1)S(1)}, bf16[768,768]{1,0:T(8,128)(2,1)}, u32[]{:S(2)}) copy-start(bf16[768,768]{1,0:T(8,128)(2,1)} %param.35) | copy-start | bytes 3538948
  4.0 43.6 %collective-permute-start = (bf16[64,256]{1,0:T(8,128)(2,1)S(1)}, bf16[64,256]{1,0:T(8,128)(2,1)S(1)}, u32[]{:S(2)}, u32[]{:S(2)}) collective-permute-start(bf16[64,256]{1,0:T(8,128)(2,1)S(1)} %get-tuple-element.123), channel_id=1, source_target_pairs={{0,1},{1,2},{2,3},{3,4},{4,5},{5,6},{6,7},{7,8},{8,9},{9,10},{10,1... | collective-permute-start | bytes 98312 | tf_op jit(solution)/shard_map/ppermute | solution.py:27
  7.7 39.9 %collective-permute-start.1 = (bf16[64,256]{1,0:T(8,128)(2,1)S(1)}, bf16[64,256]{1,0:T(8,128)(2,1)S(1)}, u32[]{:S(2)}, u32[]{:S(2)}) collective-permute-start(bf16[64,256]{1,0:T(8,128)(2,1)S(1)} %get-tuple-element.124), channel_id=1, source_target_pairs={{1,0},{2,1},{3,2},{4,3},{5,4},{6,5},{7,6},{8,7},{9,8},{10,9},{11,1... | collective-permute-start | bytes 98312 | tf_op jit(solution)/shard_map/ppermute | solution.py:28
  24.9 18.1 %copy-start.1 = (bf16[16,256,128]{2,1,0:T(8,128)(2,1)S(1)}, bf16[16,256,128]{2,1,0:T(8,128)(2,1)}, u32[]{:S(2)}) copy-start(bf16[16,256,128]{2,1,0:T(8,128)(2,1)} %param.27) | copy-start | bytes 3145732
  43.0 1.7 %copy-start.12 = (bf16[128,16]{0,1:T(8,128)(2,1)S(1)}, bf16[128,16]{0,1:T(8,128)(2,1)}, u32[]{:S(2)}) copy-start(bf16[128,16]{0,1:T(8,128)(2,1)} %param.37) | copy-start | bytes 12292
  43.0 1.7 %copy-start.13 = (f32[128]{0:T(128)S(1)}, f32[128]{0:T(128)}, u32[]{:S(2)}) copy-start(f32[128]{0:T(128)} %param.36) | copy-start | bytes 1540
  58.7 1.2 %copy-start.2 = (bf16[256,128]{1,0:T(8,128)(2,1)S(1)}, bf16[256,128]{1,0:T(8,128)(2,1)}, u32[]{:S(2)}) copy-start(bf16[256,128]{1,0:T(8,128)(2,1)} %param.21) | copy-start | bytes 196612
  58.7 1.2 %copy-start.5 = (bf16[128,128]{1,0:T(8,128)(2,1)S(1)}, bf16[128,128]{1,0:T(8,128)(2,1)}, u32[]{:S(2)}) copy-start(bf16[128,128]{1,0:T(8,128)(2,1)} %param.30) | copy-start | bytes 98308
  58.7 1.4 %copy-start.9 = (bf16[128,768]{1,0:T(8,128)(2,1)S(1)}, bf16[128,768]{1,0:T(8,128)(2,1)}, u32[]{:S(2)}) copy-start(bf16[128,768]{1,0:T(8,128)(2,1)} %param.31) | copy-start | bytes 589828
  59.2 8.7 %copy-start.8 = (s32[16]{0:T(128)S(1)}, s32[16]{0:T(128)}, u32[]{:S(2)}) copy-start(s32[16]{0:T(128)} %param.25) | copy-start | bytes 196
  59.2 8.8 %copy-start.14 = (s32[16]{0:T(128)S(1)}, s32[16]{0:T(128)}, u32[]{:S(2)}) copy-start(s32[16]{0:T(128)} %param.23) | copy-start | bytes 196
  59.2 12.8 %copy-start.10 = (bf16[32,768]{1,0:T(8,128)(2,1)S(1)}, bf16[32,768]{1,0:T(8,128)(2,1)}, u32[]{:S(2)}) copy-start(bf16[32,768]{1,0:T(8,128)(2,1)} %param.32) | copy-start | bytes 147460
  59.2 12.8 %copy-start.11 = (bf16[16,768]{1,0:T(8,128)(2,1)S(1)}, bf16[16,768]{1,0:T(8,128)(2,1)}, u32[]{:S(2)}) copy-start(bf16[16,768]{1,0:T(8,128)(2,1)} %param.26) | copy-start | bytes 73732
  59.2 12.8 %copy-start.15 = (s32[16]{0:T(128)S(1)}, s32[16]{0:T(128)}, u32[]{:S(2)}) copy-start(s32[16]{0:T(128)} %param.24) | copy-start | bytes 196
  59.2 13.3 %copy-start.6 = (f32[768]{0:T(1024)S(1)}, f32[768]{0:T(1024)}, u32[]{:S(2)}) copy-start(f32[768]{0:T(1024)} %param.33) | copy-start | bytes 9220
  60.6 7.4 %collective-permute-start.2 = (bf16[16,768]{1,0:T(8,128)(2,1)S(1)}, bf16[16,768]{1,0:T(8,128)(2,1)S(1)}, u32[]{:S(2)}, u32[]{:S(2)}) collective-permute-start(bf16[16,768]{1,0:T(8,128)(2,1)S(1)} %get-tuple-element.125), channel_id=1, source_target_pairs={{0,1},{1,2},{2,3},{3,4},{4,5},{5,6},{6,7},{7,8},{8,9},{9,10},{10,1... | collective-permute-start | bytes 73736 | tf_op jit(solution)/shard_map/ppermute | solution.py:27
  65.9 6.0 %collective-permute-start.3 = (bf16[16,768]{1,0:T(8,128)(2,1)S(1)}, bf16[16,768]{1,0:T(8,128)(2,1)S(1)}, u32[]{:S(2)}, u32[]{:S(2)}) collective-permute-start(bf16[16,768]{1,0:T(8,128)(2,1)S(1)} %get-tuple-element.126), channel_id=1, source_target_pairs={{1,0},{2,1},{3,2},{4,3},{5,4},{6,5},{7,6},{8,7},{9,8},{10,9},{11,1... | collective-permute-start | bytes 73736 | tf_op jit(solution)/shard_map/ppermute | solution.py:28
  94.5 0.7 copy-start.7
  95.5 1.1 %copy-start.3 = (bf16[768,128]{1,0:T(8,128)(2,1)S(1)}, bf16[768,128]{1,0:T(8,128)(2,1)}, u32[]{:S(2)}) copy-start(bf16[768,128]{1,0:T(8,128)(2,1)} %param.39) | copy-start | bytes 589828
  96.6 9.2 %copy-start.4 = (bf16[16,768]{1,0:T(8,128)(2,1)}, bf16[16,768]{1,0:T(8,128)(2,1)S(1)}, u32[]{:S(2)}) copy-start(bf16[16,768]{1,0:T(8,128)(2,1)S(1)} %fusion.22) | copy-start | bytes 73732
  96.8 4.3 %collective-permute-start.4 = (bf16[16,128]{1,0:T(8,128)(2,1)S(1)}, bf16[16,128]{1,0:T(8,128)(2,1)S(1)}, u32[]{:S(2)}, u32[]{:S(2)}) collective-permute-start(bf16[16,128]{1,0:T(8,128)(2,1)S(1)} %convolution_convert_fusion.2), channel_id=1, source_target_pairs={{0,1},{1,2},{2,3},{3,4},{4,5},{5,6},{6,7},{7,8},{8,9},{9,10},{10,1... | collective-permute-start | bytes 12296 | tf_op jit(solution)/shard_map/ppermute | solution.py:27
  99.2 5.8 %collective-permute-start.5 = (bf16[16,128]{1,0:T(8,128)(2,1)S(1)}, bf16[16,128]{1,0:T(8,128)(2,1)S(1)}, u32[]{:S(2)}, u32[]{:S(2)}) collective-permute-start(bf16[16,128]{1,0:T(8,128)(2,1)S(1)} %convolution_convert_fusion.2), channel_id=1, source_target_pairs={{1,0},{2,1},{3,2},{4,3},{5,4},{6,5},{7,6},{8,7},{9,8},{10,9},{11,1... | collective-permute-start | bytes 12296 | tf_op jit(solution)/shard_map/ppermute | solution.py:28
where the time goes:
time: 108 us; the launch traced here: 106 us
  local copies, waits for them, and re-layouts  32.7 us (30%)
  blocking collectives  26.1 us (24%)
  starting transfers between devices  17.2 us (16%)
  matrix products  12.8 us (12%)
  waiting for transfers between devices  7.9 us (7%)
  other arithmetic  6.81 us (6%)
  between operations  1.75 us (2%)
    gather x9, local copies, waits for them, and re-layouts, shards(): jnp.searchsorted(ends, first_atom + jnp.arange(atom_rows, dtype=jnp.int32...  17.5 us
    all_gather x1, blocking collectives, shards(): lax.all_gather(token_normed, 'row', axis=0, tiled=True)  16.4 us
    ppermute x3, starting transfers between devices, extended(): before = lax.ppermute(last, axis, up)  11.4 us
    gather x24, local copies, waits for them, and re-layouts  10.1 us
    unnamed x1, blocking collectives  9.69 us
    ppermute x3, waiting for transfers between devices, extended(): after = lax.ppermute(initial, axis, down)  7.89 us
    ppermute x3, starting transfers between devices, extended(): after = lax.ppermute(initial, axis, down)  5.78 us
    unnamed x37, local copies, waits for them, and re-layouts  3.3 us
  transfers between devices with their start and end apart: 6, of which 2 were waited for; matrix products, arithmetic and copies ran while one was open for 26% of the time, Pallas kernels for 0%

commit v1 on v0

v1 whole, which is shorter than its diff:
```python
import functools
import math

import jax
import jax.numpy as jnp
from jax import lax
from jax.experimental import pallas as pl
from jax.experimental.pallas import tpu as pltpu
from jax.sharding import PartitionSpec as P

CA = 128
CS = 768
HEADS = 16
AHEADS = 4
QBLK = 32
KWIN = 128
HDIM = 48
ADIM = 32
HALO = 64
SLAB = QBLK + 2 * HALO
LANES = 128
F32 = jnp.float32
BF16 = jnp.bfloat16


def iota(shape, dim):
    return lax.broadcasted_iota(jnp.int32, shape, dim)


def layer_norm(values, gain):
    centered = values - jnp.mean(values, axis=-1, keepdims=True)
    variance = jnp.mean(centered * centered, axis=-1, keepdims=True)
    return centered * lax.rsqrt(variance + 1e-05) * gain


def dot(a, b):
    return jnp.dot(a, b, preferred_element_type=F32)


def dot_t(a, b):
    return lax.dot_general(a, b, (((1,), (1,)), ((), ())), preferred_element_type=F32)


def kernel(
    n,
    meta_ref,
    feat_hbm,
    single_ref,
    pair_hbm,
    atom_gain_ref,
    atom_qkv_ref,
    atom_out_ref,
    pool_hbm,
    table_ref,
    token_gain_ref,
    proj_hbm,
    out_hbm,
    pair_gain_ref,
    pair_weight_ref,
    chain_weight_ref,
    back_hbm,
    atoms_out_ref,
    tokens_out_ref,
    meta_all,
    xbuf,
    pair_v,
    pool_v,
    proj_v,
    out_v,
    backw_v,
    bias_v,
    tok_all,
    back_v,
    local_sem,
    meta_send,
    meta_recv,
    halo_send,
    halo_recv,
    tok_send,
    tok_recv,
    back_send,
    back_recv,
):
    me = lax.axis_index("row")
    nxt = lax.rem(me + 1, n)
    prv = lax.rem(me + n - 1, n)
    rows = feat_hbm.shape[0]
    toks = single_ref.shape[0]
    blocks = rows // QBLK
    edge = 2 * HALO
    total_tokens = n * toks
    total_atoms = n * rows

    barrier = pltpu.get_barrier_semaphore()

    def greet(k, c):
        pl.semaphore_signal(barrier, inc=1, device_id={"row": lax.rem(me + k, n)})
        return c

    lax.fori_loop(1, n, greet, 0)

    locals_ = []
    for i, (src, dst) in enumerate(
        [
            (pair_hbm, pair_v),
            (feat_hbm, xbuf.at[pl.ds(edge, rows)]),
            (pool_hbm, pool_v),
            (proj_hbm, proj_v),
            (out_hbm, out_v),
            (back_hbm, backw_v),
        ]
    ):
        copy = pltpu.make_async_copy(src, dst, local_sem.at[i])
        copy.start()
        locals_.append(copy)
    meta_all[me] = meta_ref[...]
    back_v[...] = jnp.zeros_like(back_v)

    pl.semaphore_wait(barrier, n - 1)

    up = pltpu.make_async_remote_copy(
        src_ref=feat_hbm.at[pl.ds(rows - edge, edge)],
        dst_ref=xbuf.at[pl.ds(0, edge)],
        send_sem=halo_send.at[0],
        recv_sem=halo_recv.at[0],
        device_id={"row": nxt},
    )
    down = pltpu.make_async_remote_copy(
        src_ref=feat_hbm.at[pl.ds(0, edge)],
        dst_ref=xbuf.at[pl.ds(edge + rows, edge)],
        send_sem=halo_send.at[1],
        recv_sem=halo_recv.at[1],
        device_id={"row": prv},
    )
    up.start()
    down.start()

    def meta_copy(k, slot):
        return pltpu.make_async_remote_copy(
            src_ref=meta_ref,
            dst_ref=meta_all.at[slot],
            send_sem=meta_send.at[k],
            recv_sem=meta_recv.at[slot],
            device_id={"row": lax.rem(me + k, n)},
        )

    def tok_copy(k, slot):
        return pltpu.make_async_remote_copy(
            src_ref=tok_all.at[slot],
            dst_ref=tok_all.at[slot],
            send_sem=tok_send.at[k],
            recv_sem=tok_recv.at[slot],
            device_id={"row": lax.rem(me + k, n)},
        )

    def start_meta(k, c):
        meta_copy(k, me).start()
        return c

    lax.fori_loop(1, n, start_meta, 0)

    locals_[0].wait()
    pair_gain = pair_gain_ref[...]
    pair_weight = pair_weight_ref[...]

    def pair_step(t, c):
        normed = layer_norm(pair_v[t].astype(F32), pair_gain).astype(BF16)
        bias_v[t] = dot_t(pair_weight, normed)
        return c

    lax.fori_loop(0, toks, pair_step, 0)

    locals_[1].wait()
    up.wait_recv()
    down.wait_recv()

    def wait_meta(k, c):
        meta_copy(k, lax.rem(me + k, n)).wait_recv()
        return c

    lax.fori_loop(1, n, wait_meta, 0)

    ext = xbuf[...].astype(F32)
    normed = layer_norm(ext, atom_gain_ref[...]).astype(BF16)
    aproj = dot(normed, atom_qkv_ref[...]).astype(BF16)
    metas = {-1: meta_all[prv][0:1, :], 0: meta_all[me][0:1, :], 1: meta_all[nxt][0:1, :]}
    head_lane = iota((1, CA), 1) // ADIM
    key_lane = iota((1, SLAB), 1)
    mixed_blocks = []
    side = HALO // QBLK
    for i in range(-side, blocks + side):
        at = edge + i * QBLK
        which, inner = (-1, i + blocks) if i < 0 else ((1, i - blocks) if i >= blocks else (0, i))
        lane = 3 * toks + inner
        start = metas[which][:, lane : lane + 1]
        position = me * rows + (i * QBLK - HALO) + key_lane
        inside = (
            (position >= start)
            & (position < start + KWIN)
            & (position >= 0)
            & (position < total_atoms)
        )
        queries = aproj[at : at + QBLK, :CA]
        expanded = jnp.concatenate(
            [jnp.where(head_lane == h, queries, jnp.zeros_like(queries)) for h in range(AHEADS)],
            axis=0,
        )
        keys = aproj[at - HALO : at + QBLK + HALO, CA : 2 * CA]
        values = aproj[at - HALO : at + QBLK + HALO, 2 * CA :]
        scores = dot_t(expanded, keys) * (1.0 / math.sqrt(ADIM))
        scores = jnp.where(inside, scores, -1000000000.0)
        weights = jnp.exp(scores - jnp.max(scores, axis=-1, keepdims=True))
        denom = jnp.sum(weights, axis=-1, keepdims=True)
        full = dot(weights.astype(BF16), values) / denom
        mixed = jnp.zeros((QBLK, CA), F32)
        for h in range(AHEADS):
            mixed = jnp.where(head_lane == h, full[h * QBLK : (h + 1) * QBLK], mixed)
        mixed_blocks.append(mixed.astype(BF16))
    attended = jnp.concatenate(mixed_blocks, axis=0)
    mid = (ext[HALO : HALO + rows + 2 * HALO] + dot(attended, atom_out_ref[...])).astype(BF16)

    locals_[2].wait()
    lifted = jax.nn.relu(dot(mid, pool_v[...])).astype(BF16)

    meta_f = meta_all[:, 0, :].astype(F32)
    source = iota((n, LANES), 0)
    count_lane = iota((n, LANES), 1) < toks
    tok_row = iota((toks, LANES), 0)
    tok_lane = iota((toks, LANES), 1)

    def column(row, first):
        return jnp.sum(jnp.where(tok_lane == tok_row + first, row, 0.0), axis=1, keepdims=True)

    def spans(device, row):
        prior = jnp.where((source < device) & count_lane, meta_f, 0.0)
        prior = jnp.sum(jnp.sum(prior, axis=1, keepdims=True), axis=0, keepdims=True)
        begin = prior + jnp.sum(jnp.where(tok_lane < tok_row, row, 0.0), axis=1, keepdims=True)
        return begin, begin + column(row, 0)

    own_row = metas[0].astype(F32)
    begin, end = spans(me, own_row)
    place = (me * rows - HALO + iota((1, rows + 2 * HALO), 1)).astype(F32)
    select = ((place >= begin) & (place < end)).astype(F32).astype(BF16)
    pooled = dot(select, lifted)
    kinds = table_ref.shape[0]
    onehot = (
        (iota((toks, kinds), 1).astype(F32) == column(own_row, 2 * toks)).astype(F32).astype(BF16)
    )
    state = single_ref[...].astype(F32) + pooled / column(own_row, 0)
    state = state + dot(onehot, table_ref[...])
    token_normed = layer_norm(state, token_gain_ref[...]).astype(BF16)
    tok_all[me] = token_normed

    def start_tok(k, c):
        tok_copy(k, me).start()
        return c

    lax.fori_loop(1, n, start_tok, 0)

    locals_[3].wait()
    query = dot(token_normed, proj_v[:, :CS]).astype(BF16).astype(F32)
    gate = jax.nn.sigmoid(dot(token_normed, proj_v[:, 3 * CS :]))
    column_of = iota((HEADS, CS), 1)
    head_row = iota((HEADS, CS), 0) * HDIM
    head_mask = ((column_of >= head_row) & (column_of < head_row + HDIM)).astype(F32)
    expanded = (query[:, None, :] * head_mask[None, :, :]).reshape(toks * HEADS, CS).astype(BF16)

    shift = toks.bit_length() - 1
    token_of = iota((LANES, total_tokens), 1)
    pick = (iota((LANES, total_tokens), 0) == toks + (token_of & (toks - 1))).astype(F32)
    chains = dot(meta_f.astype(BF16), pick.astype(BF16))
    owner = iota((n, total_tokens), 1) >> shift
    chains = jnp.sum(
        jnp.where(owner == iota((n, total_tokens), 0), chains, 0.0), axis=0, keepdims=True
    )
    same = (chains == column(own_row, toks)).astype(F32)
    eye = iota((HEADS, HEADS), 0) == iota((HEADS, HEADS), 1)
    chain_weight = jnp.sum(
        jnp.where(eye, chain_weight_ref[...], 0.0), axis=1, keepdims=True
    )
    extra = bias_v[...] + same[:, None, :] * chain_weight[None, :, :]

    def wait_tok(k, c):
        tok_copy(k, lax.rem(me + k, n)).wait_recv()
        return c

    lax.fori_loop(1, n, wait_tok, 0)
    everyone = tok_all[...].reshape(total_tokens, CS)
    keys = dot(everyone, proj_v[:, CS : 2 * CS]).astype(BF16)
    scores = dot_t(expanded, keys) * (1.0 / math.sqrt(HDIM))
    scores = scores + extra.reshape(toks * HEADS, total_tokens)
    weights = jnp.exp(scores - jnp.max(scores, axis=-1, keepdims=True))
    denom = jnp.sum(weights, axis=-1, keepdims=True)
    values = dot(everyone, proj_v[:, 2 * CS : 3 * CS]).astype(BF16)
    product = dot(weights.astype(BF16), values) / denom
    mixed = jnp.sum(product.reshape(toks, HEADS, CS) * head_mask[None, :, :], axis=1)
    gated = (mixed * gate).astype(BF16)
    locals_[4].wait()
    tokens_out = (state + dot(gated, out_v[...])).astype(BF16)
    tokens_out_ref[...] = tokens_out
    locals_[5].wait()
    back = dot(tokens_out, backw_v[...]).astype(BF16)
    back_v[1] = back

    def back_copy(slot, sem, peer):
        return pltpu.make_async_remote_copy(
            src_ref=back_v.at[1],
            dst_ref=back_v.at[slot],
            send_sem=back_send.at[sem],
            recv_sem=back_recv.at[sem],
            device_id={"row": peer},
        )

    ahead = back_copy(0, 0, nxt)
    behind = back_copy(2, 1, prv)

    @pl.when(me < n - 1)
    def _():
        ahead.start()

    @pl.when(me > 0)
    def _():
        behind.start()

    place = (me * rows + iota((1, rows), 1)).astype(F32)
    selects = []
    for offset in (-1, 0, 1):
        begin, end = spans(me + offset, metas[offset].astype(F32))
        selects.append(((place >= begin) & (place < end)).astype(F32))
    select = jnp.concatenate(selects, axis=0).T.astype(BF16)

    @pl.when(me > 0)
    def _():
        ahead.wait_recv()

    @pl.when(me < n - 1)
    def _():
        behind.wait_recv()

    beside = back_v[...].reshape(3 * toks, CA)
    own_mid = mid[HALO : HALO + rows].astype(F32)
    atoms_out_ref[...] = (own_mid + dot(select, beside)).astype(BF16)

    up.wait_send()
    down.wait_send()

    def drain(k, c):
        meta_copy(k, me).wait_send()
        tok_copy(k, me).wait_send()
        return c

    lax.fori_loop(1, n, drain, 0)

    @pl.when(me < n - 1)
    def _():
        ahead.wait_send()

    @pl.when(me > 0)
    def _():
        behind.wait_send()


def shards(
    n,
    atom_feat,
    window_start,
    atom_count,
    residue_type,
    chain_id,
    token_single,
    pair,
    atom_gain,
    atom_qkv,
    atom_out,
    pool_weight,
    restype_table,
    token_gain,
    token_proj,
    token_out,
    pair_gain,
    pair_bias_weight,
    chain_weight,
    back_weight,
):
    rows, toks = atom_feat.shape[0], token_single.shape[0]
    packed = jnp.concatenate([atom_count, chain_id, residue_type, window_start])
    packed = jnp.pad(packed, (0, LANES - packed.shape[0]))
    meta = jnp.broadcast_to(packed[None, :], (8, LANES))
    vmem = pl.BlockSpec(memory_space=pltpu.VMEM)
    hbm = pl.BlockSpec(memory_space=pl.ANY)
    dma = pltpu.SemaphoreType.DMA
    return pl.pallas_call(
        functools.partial(kernel, n),
        out_shape=(
            jax.ShapeDtypeStruct((rows, CA), BF16),
            jax.ShapeDtypeStruct((toks, CS), BF16),
        ),
        in_specs=[
            vmem, hbm, vmem, hbm, vmem, vmem, vmem, hbm,
            vmem, vmem, hbm, hbm, vmem, vmem, vmem, hbm,
        ],
        out_specs=(vmem, vmem),
        scratch_shapes=[
            pltpu.VMEM((n, 8, LANES), jnp.int32),
            pltpu.VMEM((rows + 4 * HALO, CA), BF16),
            pltpu.VMEM(pair.shape, BF16),
            pltpu.VMEM(pool_weight.shape, BF16),
            pltpu.VMEM(token_proj.shape, BF16),
            pltpu.VMEM(token_out.shape, BF16),
            pltpu.VMEM(back_weight.shape, BF16),
            pltpu.VMEM((toks, HEADS, n * toks), F32),
            pltpu.VMEM((n, toks, CS), BF16),
            pltpu.VMEM((3, toks, CA), BF16),
            dma((6,)),
            dma((n,)),
            dma((n,)),
            dma((2,)),
            dma((2,)),
            dma((n,)),
            dma((n,)),
            dma((2,)),
            dma((2,)),
        ],
        compiler_params=pltpu.CompilerParams(collective_id=0, has_side_effects=True),
    )(
        meta,
        atom_feat,
        token_single,
        pair,
        atom_gain.reshape(1, -1),
        atom_qkv,
        atom_out,
        pool_weight,
        restype_table,
        token_gain.reshape(1, -1),
        token_proj,
        token_out,
        pair_gain.reshape(1, -1),
        pair_bias_weight.T,
        chain_weight.reshape(1, -1),
        back_weight,
    )


def solution(mesh):
    split = P(("groups", "row"))
    return jax.shard_map(
        functools.partial(shards, mesh.shape["row"]),
        mesh=mesh,
        in_specs=(split,) * 7 + (P(),) * 12,
        out_specs=(split, split),
        check_vma=False,
    )
```

time: 108 us -> 36.2 us (0.34); the launches traced: 106 us -> 35.7 us
  Pallas kernels: 0 us -> 29.6 us
  local copies, waits for them, and re-layouts: 32.7 us -> 4.69 us
  blocking collectives: 26.1 us -> 0 us
  starting transfers between devices: 17.2 us -> 0 us
  matrix products: 12.8 us -> 0 us
  waiting for transfers between devices: 7.9 us -> 0 us
  other arithmetic: 6.81 us -> 0.78 us
  between operations: 1.75 us -> 0.64 us
    pallas_call x0 -> x1, Pallas kernels: none -> 29.6 us  [shards(): pl.pallas_call(functools.partial(kernel, n), out_shape=(jax.ShapeDtypeStr...]
    gather x33 -> x0, local copies, waits for them, and re-layouts: 27.5 us -> none  [the longest x9 17.5 us: shards(): jnp.searchsorted(ends, first_atom + jnp.arange(atom_rows, dtype=jnp.int32...]
    ppermute x6 -> x0, starting transfers between devices: 17.2 us -> none  [the longest x3 11.4 us: extended(): before = lax.ppermute(last, axis, up)]
    all_gather x1 -> x0, blocking collectives: 16.4 us -> none  [shards(): lax.all_gather(token_normed, 'row', axis=0, tiled=True)]
    dot_general x14 -> x0, matrix products: 12.8 us -> none  [the longest x1 3.06 us: shards(): jnp.dot(token_normed, token_proj, preferred_element_type=jnp.float32)]
    unnamed x1 -> x0, blocking collectives: 9.69 us -> none
    ppermute x6 -> x0, waiting for transfers between devices: 7.9 us -> none  [the longest x3 7.89 us: extended(): after = lax.ppermute(initial, axis, down)]
    reduce_sum x7 -> x0, other arithmetic: 4.51 us -> none  [the longest x3 2.51 us: layer_norm(): variance = jnp.mean(centered * centered, axis=-1, keepdims=True)]
  transfers between devices with their start and end apart: 6 -> 0, of which waited for: 2 -> 0; matrix products, arithmetic and copies ran while one was open for 26% -> 0% of each run, Pallas kernels for 0% -> 0%
where the time goes in v1:
time: 36.2 us; the launch traced here: 35.7 us
  Pallas kernels  29.6 us (82%)
  local copies, waits for them, and re-layouts  4.69 us (13%)
  other arithmetic  0.78 us (2%)
  between operations  0.64 us (2%)
    pallas_call x1, Pallas kernels, shards(): pl.pallas_call(functools.partial(kernel, n), out_shape=(jax.ShapeDtypeStr...  29.6 us
    unnamed x2, local copies, waits for them, and re-layouts  2.82 us
    reshape x1, local copies, waits for them, and re-layouts, shards(): token_gain.reshape(1, -1)  1.27 us
    concatenate x1, other arithmetic, shards(): packed = jnp.concatenate([atom_count, chain_id, residue_type, window_start])  0.78 us

profile of v1, /device:TPU:5, one launch (start us, length us, event | category | flops | bytes accessed | tf_op | source)
XLA Modules:
  0.0 35.7 jit_solution(5735877982129281807)
XLA Ops:
  0.6 0.8 %pad_add_fusion = s32[56]{0:T(128)S(1)} fusion(s32[8]{0:T(128)} %param.20, s32[16]{0:T(128)} %param.22, s32[16]{0:T(128)} %param.23, s32[16]{0:T(128)} %param.21), kind=kLoop, calls=%fused_computation | loop fusion | flops 168 | bytes 448 | tf_op jit(solution)/shard_map/concatenate | solution.py:386
  1.4 1.3 %reshape.18.token_gain_ref = f32[1,768]{1,0:T(1,128)} reshape(f32[768]{0:T(1024)} %param.31) | data formatting | bytes 6144 | tf_op jit(solution)/shard_map/reshape | solution.py:435
  2.7 0.6 %broadcast_in_dim.2.meta_ref = s32[8,128]{1,0:T(8,128)} broadcast(s32[128]{0:T(128)S(1)} %pad.4), dimensions={1} | broadcast | bytes 4608 | tf_op jit(solution)/shard_map/broadcast_in_dim | solution.py:388
  3.3 29.6 %shard_map.194 = (bf16[256,128]{1,0:T(8,128)(2,1)}, bf16[16,768]{1,0:T(8,128)(2,1)}) custom-call(s32[8,128]{1,0:T(8,128)} %broadcast_in_dim.2.meta_ref, bf16[256,128]{1,0:T(8,128)(2,1)} %feat_hbm.1, bf16[16,768]{1,0:T(8,128)(2,1)} %single_ref.1, bf16[16,256,128]{2,1,0:T(8,128)(2,1)} %pair_hbm.1, f32[1,128]{1,0:T(1,128)} %bitcast.5, ...), custom_call_target="tpu_custom_call" | custom-call | tf_op jit(solution)/shard_map/pallas_call | solution.py:392
  32.8 1.5 %copy.23 = bf16[256,128]{1,0:T(8,128)(2,1)} copy(bf16[256,128]{1,0:T(8,128)(2,1)} %get-tuple-element.4) | data formatting | bytes 131072
  34.3 1.3 %copy.24 = bf16[16,768]{1,0:T(8,128)(2,1)} copy(bf16[16,768]{1,0:T(8,128)(2,1)} %get-tuple-element.5) | data formatting | bytes 49152
  (1 shorter events, 0.0 us)

commit v2 on v1

--- a/solution.py
+++ b/solution.py
@@ -41,51 +41,57 @@
     return lax.dot_general(a, b, (((1,), (1,)), ((), ())), preferred_element_type=F32)
 
 
-def kernel(
-    n,
-    meta_ref,
-    feat_hbm,
-    single_ref,
-    pair_hbm,
-    atom_gain_ref,
-    atom_qkv_ref,
-    atom_out_ref,
-    pool_hbm,
-    table_ref,
-    token_gain_ref,
-    proj_hbm,
-    out_hbm,
-    pair_gain_ref,
-    pair_weight_ref,
-    chain_weight_ref,
-    back_hbm,
-    atoms_out_ref,
-    tokens_out_ref,
-    meta_all,
-    xbuf,
-    pair_v,
-    pool_v,
-    proj_v,
-    out_v,
-    backw_v,
-    bias_v,
-    tok_all,
-    back_v,
-    local_sem,
-    meta_send,
-    meta_recv,
-    halo_send,
-    halo_recv,
-    tok_send,
-    tok_recv,
-    back_send,
-    back_recv,
-):
+NAMES = (
+        "feat",
+        "window",
+        "count",
+        "residue",
+        "chain",
+        "single",
+        "pair",
+        "atom_gain",
+        "atom_qkv",
+        "atom_out",
+        "pool",
+        "table",
+        "token_gain",
+        "proj",
+        "out",
+        "pair_gain",
+        "pair_weight",
+        "chain_weight",
+        "back",
+    )
+
+
+def kernel(n, *refs):
+    count = len(NAMES)
+    hbm = dict(zip(NAMES, refs[:count]))
+    atoms_out_ref, tokens_out_ref = refs[count : count + 2]
+    v = dict(zip(NAMES, refs[count + 2 : 2 * count + 2]))
+    (
+        stage,
+        meta_all,
+        bias_v,
+        tok_all,
+        back_v,
+        local_sem,
+        meta_send,
+        meta_recv,
+        halo_send,
+        halo_recv,
+        tok_send,
+        tok_recv,
+        back_send,
+        back_recv,
+    ) = refs[2 * count + 2 :]
+    xbuf = v["feat"]
+    feat_hbm = hbm["feat"]
     me = lax.axis_index("row")
     nxt = lax.rem(me + 1, n)
     prv = lax.rem(me + n - 1, n)
     rows = feat_hbm.shape[0]
-    toks = single_ref.shape[0]
+    toks = hbm["single"].shape[0]
     blocks = rows // QBLK
     edge = 2 * HALO
     total_tokens = n * toks
@@ -99,23 +105,53 @@
 
     lax.fori_loop(1, n, greet, 0)
 
-    locals_ = []
-    for i, (src, dst) in enumerate(
-        [
-            (pair_hbm, pair_v),
-            (feat_hbm, xbuf.at[pl.ds(edge, rows)]),
-            (pool_hbm, pool_v),
-            (proj_hbm, proj_v),
-            (out_hbm, out_v),
-            (back_hbm, backw_v),
-        ]
-    ):
-        copy = pltpu.make_async_copy(src, dst, local_sem.at[i])
-        copy.start()
-        locals_.append(copy)
-    meta_all[me] = meta_ref[...]
+    loads = {}
+    order = (
+        "pair",
+        "pair_gain",
+        "pair_weight",
+        "count",
+        "chain",
+        "window",
+        "residue",
+        "feat",
+        "atom_gain",
+        "atom_qkv",
+        "atom_out",
+        "pool",
+        "single",
+        "table",
+        "token_gain",
+        "chain_weight",
+        "proj",
+        "out",
+        "back",
+    )
+    for i, name in enumerate(order):
+        dst = xbuf.at[pl.ds(edge, rows)] if name == "feat" else v[name]
+        loads[name] = pltpu.make_async_copy(hbm[name], dst, local_sem.at[i])
+        loads[name].start()
     back_v[...] = jnp.zeros_like(back_v)
-
+    stage[...] = jnp.zeros_like(stage)
+    for i, name in enumerate(("count", "chain", "window", "residue")):
+        loads[name].wait()
+        value = v[name][...]
+        stage[i : i + 1, : value.shape[1]] = value
+    meta_all[me] = stage[...]
+
+    loads["pair"].wait()
+    loads["pair_gain"].wait()
+    loads["pair_weight"].wait()
+    pair_gain = v["pair_gain"][...]
+    pair_weight = v["pair_weight"][...]
+
+    def pair_step(t, c):
+        normed = layer_norm(v["pair"][t].astype(F32), pair_gain).astype(BF16)
+        bias_v[t] = dot_t(pair_weight, normed)
+        return c
+
+    first, second = toks // 4, toks // 2
+    lax.fori_loop(0, first, pair_step, 0, unroll=4)
     pl.semaphore_wait(barrier, n - 1)
 
     up = pltpu.make_async_remote_copy(
@@ -137,7 +173,7 @@
 
     def meta_copy(k, slot):
         return pltpu.make_async_remote_copy(
-            src_ref=meta_ref,
+            src_ref=stage,
             dst_ref=meta_all.at[slot],
             send_sem=meta_send.at[k],
             recv_sem=meta_recv.at[slot],
@@ -159,18 +195,10 @@
 
     lax.fori_loop(1, n, start_meta, 0)
 
-    locals_[0].wait()
-    pair_gain = pair_gain_ref[...]
-    pair_weight = pair_weight_ref[...]
-
-    def pair_step(t, c):
-        normed = layer_norm(pair_v[t].astype(F32), pair_gain).astype(BF16)
-        bias_v[t] = dot_t(pair_weight, normed)
-        return c
-
-    lax.fori_loop(0, toks, pair_step, 0)
-
-    locals_[1].wait()
+    lax.fori_loop(first, second, pair_step, 0, unroll=4)
+
+    for name in ("feat", "atom_gain", "atom_qkv", "atom_out", "pool"):
+        loads[name].wait()
     up.wait_recv()
     down.wait_recv()
 
@@ -181,9 +209,9 @@
     lax.fori_loop(1, n, wait_meta, 0)
 
     ext = xbuf[...].astype(F32)
-    normed = layer_norm(ext, atom_gain_ref[...]).astype(BF16)
-    aproj = dot(normed, atom_qkv_ref[...]).astype(BF16)
-    metas = {-1: meta_all[prv][0:1, :], 0: meta_all[me][0:1, :], 1: meta_all[nxt][0:1, :]}
+    normed = layer_norm(ext, v["atom_gain"][...]).astype(BF16)
+    aproj = dot(normed, v["atom_qkv"][...]).astype(BF16)
+    metas = {-1: meta_all[prv], 0: meta_all[me], 1: meta_all[nxt]}
     head_lane = iota((1, CA), 1) // ADIM
     key_lane = iota((1, SLAB), 1)
     mixed_blocks = []
@@ -191,8 +219,7 @@
     for i in range(-side, blocks + side):
         at = edge + i * QBLK
         which, inner = (-1, i + blocks) if i < 0 else ((1, i - blocks) if i >= blocks else (0, i))
-        lane = 3 * toks + inner
-        start = metas[which][:, lane : lane + 1]
+        start = metas[which][2:3, inner : inner + 1]
         position = me * rows + (i * QBLK - HALO) + key_lane
         inside = (
             (position >= start)
@@ -217,38 +244,42 @@
             mixed = jnp.where(head_lane == h, full[h * QBLK : (h + 1) * QBLK], mixed)
         mixed_blocks.append(mixed.astype(BF16))
     attended = jnp.concatenate(mixed_blocks, axis=0)
-    mid = (ext[HALO : HALO + rows + 2 * HALO] + dot(attended, atom_out_ref[...])).astype(BF16)
-
-    locals_[2].wait()
-    lifted = jax.nn.relu(dot(mid, pool_v[...])).astype(BF16)
-
-    meta_f = meta_all[:, 0, :].astype(F32)
+    mid = (ext[HALO : HALO + rows + 2 * HALO] + dot(attended, v["atom_out"][...])).astype(BF16)
+
+    lifted = jax.nn.relu(dot(mid, v["pool"][...])).astype(BF16)
+
+    counts_f = meta_all[:, 0, :].astype(F32)
     source = iota((n, LANES), 0)
     count_lane = iota((n, LANES), 1) < toks
     tok_row = iota((toks, LANES), 0)
     tok_lane = iota((toks, LANES), 1)
 
-    def column(row, first):
-        return jnp.sum(jnp.where(tok_lane == tok_row + first, row, 0.0), axis=1, keepdims=True)
+    def column(row):
+        return jnp.sum(jnp.where(tok_lane == tok_row, row, 0.0), axis=1, keepdims=True)
 
     def spans(device, row):
-        prior = jnp.where((source < device) & count_lane, meta_f, 0.0)
+        prior = jnp.where((source < device) & count_lane, counts_f, 0.0)
         prior = jnp.sum(jnp.sum(prior, axis=1, keepdims=True), axis=0, keepdims=True)
         begin = prior + jnp.sum(jnp.where(tok_lane < tok_row, row, 0.0), axis=1, keepdims=True)
-        return begin, begin + column(row, 0)
-
-    own_row = metas[0].astype(F32)
+        return begin, begin + column(row)
+
+    own_meta = metas[0].astype(F32)
+    own_row = own_meta[0:1]
     begin, end = spans(me, own_row)
     place = (me * rows - HALO + iota((1, rows + 2 * HALO), 1)).astype(F32)
     select = ((place >= begin) & (place < end)).astype(F32).astype(BF16)
     pooled = dot(select, lifted)
-    kinds = table_ref.shape[0]
+    kinds = hbm["table"].shape[0]
     onehot = (
-        (iota((toks, kinds), 1).astype(F32) == column(own_row, 2 * toks)).astype(F32).astype(BF16)
-    )
-    state = single_ref[...].astype(F32) + pooled / column(own_row, 0)
-    state = state + dot(onehot, table_ref[...])
-    token_normed = layer_norm(state, token_gain_ref[...]).astype(BF16)
+        (iota((toks, kinds), 1).astype(F32) == column(own_meta[3:4])).astype(F32).astype(BF16)
+    )
+    for name in ("single", "table", "token_gain", "chain_weight"):
+        loads[name].wait()
+    state = v["single"][...].astype(F32) + pooled / column(own_row)
+    state = state + dot(onehot, v["table"][...])
+    gain = v["token_gain"][...]
+    gain = jnp.concatenate([gain[i : i + 1] for i in range(gain.shape[0])], axis=1)
+    token_normed = layer_norm(state, gain).astype(BF16)
     tok_all[me] = token_normed
 
     def start_tok(k, c):
@@ -257,7 +288,8 @@
 
     lax.fori_loop(1, n, start_tok, 0)
 
-    locals_[3].wait()
+    loads["proj"].wait()
+    proj_v = v["proj"]
     query = dot(token_normed, proj_v[:, :CS]).astype(BF16).astype(F32)
     gate = jax.nn.sigmoid(dot(token_normed, proj_v[:, 3 * CS :]))
     column_of = iota((HEADS, CS), 1)
@@ -267,17 +299,18 @@
 
     shift = toks.bit_length() - 1
     token_of = iota((LANES, total_tokens), 1)
-    pick = (iota((LANES, total_tokens), 0) == toks + (token_of & (toks - 1))).astype(F32)
-    chains = dot(meta_f.astype(BF16), pick.astype(BF16))
+    pick = (iota((LANES, total_tokens), 0) == (token_of & (toks - 1))).astype(F32)
+    chains = dot(meta_all[:, 1, :].astype(F32).astype(BF16), pick.astype(BF16))
     owner = iota((n, total_tokens), 1) >> shift
     chains = jnp.sum(
         jnp.where(owner == iota((n, total_tokens), 0), chains, 0.0), axis=0, keepdims=True
     )
-    same = (chains == column(own_row, toks)).astype(F32)
+    same = (chains == column(own_meta[1:2])).astype(F32)
     eye = iota((HEADS, HEADS), 0) == iota((HEADS, HEADS), 1)
     chain_weight = jnp.sum(
-        jnp.where(eye, chain_weight_ref[...], 0.0), axis=1, keepdims=True
-    )
+        jnp.where(eye, v["chain_weight"][...], 0.0), axis=1, keepdims=True
+    )
+    lax.fori_loop(second, toks, pair_step, 0, unroll=4)
     extra = bias_v[...] + same[:, None, :] * chain_weight[None, :, :]
 
     def wait_tok(k, c):
@@ -295,11 +328,11 @@
     product = dot(weights.astype(BF16), values) / denom
     mixed = jnp.sum(product.reshape(toks, HEADS, CS) * head_mask[None, :, :], axis=1)
     gated = (mixed * gate).astype(BF16)
-    locals_[4].wait()
-    tokens_out = (state + dot(gated, out_v[...])).astype(BF16)
+    loads["out"].wait()
+    tokens_out = (state + dot(gated, v["out"][...])).astype(BF16)
     tokens_out_ref[...] = tokens_out
-    locals_[5].wait()
-    back = dot(tokens_out, backw_v[...]).astype(BF16)
+    loads["back"].wait()
+    back = dot(tokens_out, v["back"][...]).astype(BF16)
     back_v[1] = back
 
     def back_copy(slot, sem, peer):
@@ -325,7 +358,7 @@
     place = (me * rows + iota((1, rows), 1)).astype(F32)
     selects = []
     for offset in (-1, 0, 1):
-        begin, end = spans(me + offset, metas[offset].astype(F32))
+        begin, end = spans(me + offset, metas[offset][0:1].astype(F32))
         selects.append(((place >= begin) & (place < end)).astype(F32))
     select = jnp.concatenate(selects, axis=0).T.astype(BF16)
 
@@ -383,35 +416,48 @@
     back_weight,
 ):
     rows, toks = atom_feat.shape[0], token_single.shape[0]
-    packed = jnp.concatenate([atom_count, chain_id, residue_type, window_start])
-    packed = jnp.pad(packed, (0, LANES - packed.shape[0]))
-    meta = jnp.broadcast_to(packed[None, :], (8, LANES))
+    args = [
+        atom_feat,
+        window_start.reshape(1, -1),
+        atom_count.reshape(1, -1),
+        residue_type.reshape(1, -1),
+        chain_id.reshape(1, -1),
+        token_single,
+        pair,
+        atom_gain.reshape(1, -1),
+        atom_qkv,
+        atom_out,
+        pool_weight,
+        restype_table,
+        token_gain.reshape(-1, LANES),
+        token_proj,
+        token_out,
+        pair_gain.reshape(1, -1),
+        pair_bias_weight.T,
+        chain_weight.reshape(1, -1),
+        back_weight,
+    ]
     vmem = pl.BlockSpec(memory_space=pltpu.VMEM)
-    hbm = pl.BlockSpec(memory_space=pl.ANY)
     dma = pltpu.SemaphoreType.DMA
-    return pl.pallas_call(
+    held = [pltpu.VMEM(x.shape, x.dtype) for x in args]
+    held[0] = pltpu.VMEM((rows + 4 * HALO, CA), BF16)
+    shapes = (
+        jax.ShapeDtypeStruct((rows, CA), BF16),
+        jax.ShapeDtypeStruct((toks, CS), BF16),
+    )
+    results = pl.pallas_call(
         functools.partial(kernel, n),
-        out_shape=(
-            jax.ShapeDtypeStruct((rows, CA), BF16),
-            jax.ShapeDtypeStruct((toks, CS), BF16),
-        ),
-        in_specs=[
-            vmem, hbm, vmem, hbm, vmem, vmem, vmem, hbm,
-            vmem, vmem, hbm, hbm, vmem, vmem, vmem, hbm,
-        ],
+        out_shape=shapes,
+        in_specs=[pl.BlockSpec(memory_space=pltpu.HBM)] * len(args),
         out_specs=(vmem, vmem),
-        scratch_shapes=[
+        scratch_shapes=held
+        + [
+            pltpu.VMEM((8, LANES), jnp.int32),
             pltpu.VMEM((n, 8, LANES), jnp.int32),
-            pltpu.VMEM((rows + 4 * HALO, CA), BF16),
-            pltpu.VMEM(pair.shape, BF16),
-            pltpu.VMEM(pool_weight.shape, BF16),
-            pltpu.VMEM(token_proj.shape, BF16),
-            pltpu.VMEM(token_out.shape, BF16),
-            pltpu.VMEM(back_weight.shape, BF16),
             pltpu.VMEM((toks, HEADS, n * toks), F32),
             pltpu.VMEM((n, toks, CS), BF16),
             pltpu.VMEM((3, toks, CA), BF16),
-            dma((6,)),
+            dma((len(args),)),
             dma((n,)),
             dma((n,)),
             dma((2,)),
@@ -421,25 +467,22 @@
             dma((2,)),
             dma((2,)),
         ],
-        compiler_params=pltpu.CompilerParams(collective_id=0, has_side_effects=True),
-    )(
-        meta,
-        atom_feat,
-        token_single,
-        pair,
-        atom_gain.reshape(1, -1),
-        atom_qkv,
-        atom_out,
-        pool_weight,
-        restype_table,
-        token_gain.reshape(1, -1),
-        token_proj,
-        token_out,
-        pair_gain.reshape(1, -1),
-        pair_bias_weight.T,
-        chain_weight.reshape(1, -1),
-        back_weight,
-    )
+        compiler_params=pltpu.CompilerParams(
+            collective_id=0, has_side_effects=True
+        ),
+    )(*args)
+    return pl.pallas_call(
+        hand_over,
+        out_shape=shapes,
+        in_specs=[vmem, vmem],
+        out_specs=(vmem, vmem),
+        compiler_params=pltpu.CompilerParams(vmem_limit_bytes=4 << 20),
+    )(*results)
+
+
+def hand_over(atoms_ref, tokens_ref, atoms_out_ref, tokens_out_ref):
+    atoms_out_ref[...] = atoms_ref[...]
+    tokens_out_ref[...] = tokens_ref[...]
 
 
 def solution(mesh):

time: 36.2 us -> 31.9 us (0.88)
  local copies, waits for them, and re-layouts: 4.69 us -> 1.57 us
  other arithmetic: 0.78 us -> 0 us
    reshape x1 -> x0, local copies, waits for them, and re-layouts: 1.27 us -> none  [shards(): token_gain.reshape(1, -1)]
    unnamed x2 -> x4, local copies, waits for them, and re-layouts: 2.82 us -> 1.57 us
    concatenate x1 -> x0, other arithmetic: 0.78 us -> none  [shards(): packed = jnp.concatenate([atom_count, chain_id, residue_type, window_start])]
    broadcast_in_dim x1 -> x0, local copies, waits for them, and re-layouts: 0.59 us -> none  [shards(): meta = jnp.broadcast_to(packed[None, :], (8, LANES))]
    pallas_call x1 -> x2, Pallas kernels: 29.6 us -> 29.5 us  [the longest x1 28.9 us: shards(): pl.pallas_call(functools.partial(kernel, n), out_shape=shapes, in_specs=[...]
where the time goes in v2:
time: 31.9 us; the launch traced here: 31.7 us
  Pallas kernels  29.5 us (92%)
  local copies, waits for them, and re-layouts  1.57 us (5%)
  between operations  0.66 us (2%)
    pallas_call x1, Pallas kernels, shards(): pl.pallas_call(functools.partial(kernel, n), out_shape=shapes, in_specs=[...  28.9 us
    unnamed x4, local copies, waits for them, and re-layouts  1.57 us

profile of v2, /device:TPU:5, one launch (start us, length us, event | category | flops | bytes accessed | tf_op | source)
XLA Modules:
  0.0 31.7 jit_solution(8612983909908847841)
XLA Ops:
  0.6 28.9 %shard_map.194 = (bf16[256,128]{1,0:T(8,128)(2,1)}, bf16[16,768]{1,0:T(8,128)(2,1)}) custom-call(bf16[256,128]{1,0:T(8,128)(2,1)} %refs_0_.1, s32[1,8]{1,0:T(1,128)} %bitcast.11, s32[1,16]{1,0:T(1,128)} %bitcast.12, s32[1,16]{1,0:T(1,128)} %bitcast.13, s32[1,16]{1,0:T(1,128)} %bitcast.14, bf16[16,768]{1,0:T(8,128)(2,1)} %refs_5_.1, ...), custom_call_target="tpu_custom_call" | custom-call | tf_op jit(solution)/shard_map/pallas_call | solution.py:448
  29.5 0.0 copy-start
  29.5 0.8 %copy-done = bf16[256,128]{1,0:T(8,128)(2,1)S(1)} copy-done((bf16[256,128]{1,0:T(8,128)(2,1)S(1)}, bf16[256,128]{1,0:T(8,128)(2,1)}, u32[]{:S(2)}) %copy-start) | copy-done | bytes 65560
  30.3 0.0 copy-start.1
  30.3 0.7 %copy-done.1 = bf16[16,768]{1,0:T(8,128)(2,1)S(1)} copy-done((bf16[16,768]{1,0:T(8,128)(2,1)S(1)}, bf16[16,768]{1,0:T(8,128)(2,1)}, u32[]{:S(2)}) %copy-start.1) | copy-done | bytes 24600
  31.1 0.6 %shard_map.195 = (bf16[256,128]{1,0:T(8,128)(2,1)}, bf16[16,768]{1,0:T(8,128)(2,1)}) custom-call(bf16[256,128]{1,0:T(8,128)(2,1)S(1)} %copy-done, bf16[16,768]{1,0:T(8,128)(2,1)S(1)} %copy-done.1), custom_call_target="tpu_custom_call" | custom-call | tf_op jit(solution)/shard_map/pallas_call | solution.py:474
Async XLA Ops:
  29.5 0.8 %copy-start = (bf16[256,128]{1,0:T(8,128)(2,1)S(1)}, bf16[256,128]{1,0:T(8,128)(2,1)}, u32[]{:S(2)}) copy-start(bf16[256,128]{1,0:T(8,128)(2,1)} %get-tuple-element.4.atoms_ref) | copy-start | bytes 196612
  30.3 0.7 %copy-start.1 = (bf16[16,768]{1,0:T(8,128)(2,1)S(1)}, bf16[16,768]{1,0:T(8,128)(2,1)}, u32[]{:S(2)}) copy-start(bf16[16,768]{1,0:T(8,128)(2,1)} %get-tuple-element.5.tokens_ref) | copy-start | bytes 73732

commit v3 on v2

--- a/solution.py
+++ b/solution.py
@@ -17,7 +17,6 @@
 HDIM = 48
 ADIM = 32
 HALO = 64
-SLAB = QBLK + 2 * HALO
 LANES = 128
 F32 = jnp.float32
 BF16 = jnp.bfloat16
@@ -150,8 +149,52 @@
         bias_v[t] = dot_t(pair_weight, normed)
         return c
 
-    first, second = toks // 4, toks // 2
-    lax.fori_loop(0, first, pair_step, 0, unroll=4)
+    for name in ("feat", "atom_gain", "atom_qkv"):
+        loads[name].wait()
+    head_lane = iota((1, CA), 1) // ADIM
+
+    def project(values):
+        normed = layer_norm(values.astype(F32), v["atom_gain"][...]).astype(BF16)
+        return dot(normed, v["atom_qkv"][...]).astype(BF16)
+
+    def attend(first_atom, starts, queries, keyvals):
+        position = me * rows + (first_atom - HALO) + iota((edge, 2 * edge), 1)
+        inside = (
+            (position >= starts)
+            & (position < starts + KWIN)
+            & (position >= 0)
+            & (position < total_atoms)
+        )
+        mixed = jnp.zeros((edge, CA), F32)
+        for h in range(AHEADS):
+            masked = jnp.where(head_lane == h, queries, jnp.zeros_like(queries))
+            scores = dot_t(masked, keyvals[:, :CA]) * (1.0 / math.sqrt(ADIM))
+            scores = jnp.where(inside, scores, -1000000000.0)
+            weights = jnp.exp(scores - jnp.max(scores, axis=-1, keepdims=True))
+            denom = jnp.sum(weights, axis=-1, keepdims=True)
+            full = dot(weights.astype(BF16), keyvals[:, CA:]) / denom
+            mixed = jnp.where(head_lane == h, full, mixed)
+        return mixed.astype(BF16)
+
+    def starts_of(pieces):
+        return jnp.concatenate([jnp.broadcast_to(x, (QBLK, 1)) for x in pieces], axis=0)
+
+    own_proj = project(xbuf[edge : edge + rows])
+    own_window = v["window"][...]
+    per = edge // QBLK
+    side = HALO // QBLK
+    groups = {}
+    for g in range(1, rows // edge):
+        at = g * edge - HALO
+        first_block = at // QBLK
+        starts = starts_of(
+            [own_window[:, i : i + 1] for i in range(first_block, first_block + per)]
+        )
+        groups[g] = attend(
+            at, starts, own_proj[at : at + edge, :CA], own_proj[at - HALO : at + edge + HALO, CA:]
+        )
+
+    first, second = 0, toks // 4
     pl.semaphore_wait(barrier, n - 1)
 
     up = pltpu.make_async_remote_copy(
@@ -180,14 +223,43 @@
             device_id={"row": lax.rem(me + k, n)},
         )
 
-    def tok_copy(k, slot):
+    lines = n // 4
+    line, seat = lax.div(me, 4), lax.rem(me, 4)
+    across = me + 2 - 4 * lax.rem(lax.div(me, 2), 2)
+    sibling = me + 1 - 2 * lax.rem(me, 2)
+    across_seat = lax.rem(across, 4)
+    sibling_seat = lax.rem(sibling, 4)
+    corner_seat = 3 - seat
+
+    def slot_of(k, place):
+        return 4 * lax.rem(line + k, lines) + place
+
+    def tok_copy(sem, slot, peer):
         return pltpu.make_async_remote_copy(
             src_ref=tok_all.at[slot],
             dst_ref=tok_all.at[slot],
-            send_sem=tok_send.at[k],
+            send_sem=tok_send.at[sem],
             recv_sem=tok_recv.at[slot],
-            device_id={"row": lax.rem(me + k, n)},
+            device_id={"row": peer},
         )
+
+    def along_line(k):
+        return tok_copy(k, me, slot_of(k, seat))
+
+    def to_across(k):
+        return tok_copy(lines + k, slot_of(k, seat), across)
+
+    def to_sibling(k):
+        return tok_copy(2 * lines + k, slot_of(k, seat), sibling)
+
+    def corner(k):
+        return tok_copy(3 * lines + k, slot_of(k, across_seat), sibling)
+
+    def diagonal(k):
+        return tok_copy(lines + k, me, slot_of(k, across_seat))
+
+    def arrived(k, place):
+        tok_copy(0, slot_of(k, place), sibling).wait_recv()
 
     def start_meta(k, c):
         meta_copy(k, me).start()
@@ -197,7 +269,7 @@
 
     lax.fori_loop(first, second, pair_step, 0, unroll=4)
 
-    for name in ("feat", "atom_gain", "atom_qkv", "atom_out", "pool"):
+    for name in ("atom_out", "pool"):
         loads[name].wait()
     up.wait_recv()
     down.wait_recv()
@@ -206,45 +278,29 @@
         meta_copy(k, lax.rem(me + k, n)).wait_recv()
         return c
 
-    lax.fori_loop(1, n, wait_meta, 0)
-
-    ext = xbuf[...].astype(F32)
-    normed = layer_norm(ext, v["atom_gain"][...]).astype(BF16)
-    aproj = dot(normed, v["atom_qkv"][...]).astype(BF16)
+    wait_meta(1, 0)
+    wait_meta(n - 1, 0)
     metas = {-1: meta_all[prv], 0: meta_all[me], 1: meta_all[nxt]}
-    head_lane = iota((1, CA), 1) // ADIM
-    key_lane = iota((1, SLAB), 1)
-    mixed_blocks = []
-    side = HALO // QBLK
-    for i in range(-side, blocks + side):
-        at = edge + i * QBLK
-        which, inner = (-1, i + blocks) if i < 0 else ((1, i - blocks) if i >= blocks else (0, i))
-        start = metas[which][2:3, inner : inner + 1]
-        position = me * rows + (i * QBLK - HALO) + key_lane
-        inside = (
-            (position >= start)
-            & (position < start + KWIN)
-            & (position >= 0)
-            & (position < total_atoms)
-        )
-        queries = aproj[at : at + QBLK, :CA]
-        expanded = jnp.concatenate(
-            [jnp.where(head_lane == h, queries, jnp.zeros_like(queries)) for h in range(AHEADS)],
-            axis=0,
-        )
-        keys = aproj[at - HALO : at + QBLK + HALO, CA : 2 * CA]
-        values = aproj[at - HALO : at + QBLK + HALO, 2 * CA :]
-        scores = dot_t(expanded, keys) * (1.0 / math.sqrt(ADIM))
-        scores = jnp.where(inside, scores, -1000000000.0)
-        weights = jnp.exp(scores - jnp.max(scores, axis=-1, keepdims=True))
-        denom = jnp.sum(weights, axis=-1, keepdims=True)
-        full = dot(weights.astype(BF16), values) / denom
-        mixed = jnp.zeros((QBLK, CA), F32)
-        for h in range(AHEADS):
-            mixed = jnp.where(head_lane == h, full[h * QBLK : (h + 1) * QBLK], mixed)
-        mixed_blocks.append(mixed.astype(BF16))
-    attended = jnp.concatenate(mixed_blocks, axis=0)
-    mid = (ext[HALO : HALO + rows + 2 * HALO] + dot(attended, v["atom_out"][...])).astype(BF16)
+    low = project(xbuf[:edge])
+    starts = starts_of(
+        [metas[-1][2:3, i : i + 1] for i in range(blocks - side, blocks)]
+        + [own_window[:, i : i + 1] for i in range(per - side)]
+    )
+    keyvals = jnp.concatenate([low[:, CA:], own_proj[:edge, CA:]], axis=0)
+    queries = jnp.concatenate([low[edge - HALO :, :CA], own_proj[: edge - HALO, :CA]], axis=0)
+    groups[0] = attend(-HALO, starts, queries, keyvals)
+    high = project(xbuf[edge + rows :])
+    starts = starts_of(
+        [own_window[:, i : i + 1] for i in range(blocks - per + side, blocks)]
+        + [metas[1][2:3, i : i + 1] for i in range(side)]
+    )
+    keyvals = jnp.concatenate([own_proj[rows - edge :, CA:], high[:, CA:]], axis=0)
+    queries = jnp.concatenate([own_proj[rows - edge + HALO :, :CA], high[:HALO, :CA]], axis=0)
+    groups[rows // edge] = attend(rows - edge + HALO, starts, queries, keyvals)
+    ext = xbuf[HALO : 3 * HALO + rows].astype(F32)
+    lax.fori_loop(2, n - 1, wait_meta, 0)
+    attended = jnp.concatenate([groups[g] for g in range(rows // edge + 1)], axis=0)
+    mid = (ext + dot(attended, v["atom_out"][...])).astype(BF16)
 
     lifted = jax.nn.relu(dot(mid, v["pool"][...])).astype(BF16)
 
@@ -283,10 +339,13 @@
     tok_all[me] = token_normed
 
     def start_tok(k, c):
-        tok_copy(k, me).start()
-        return c
-
-    lax.fori_loop(1, n, start_tok, 0)
+        along_line(k).start()
+        diagonal(k).start()
+        return c
+
+    lax.fori_loop(1, lines, start_tok, 0)
+    to_across(0).start()
+    to_sibling(0).start()
 
     loads["proj"].wait()
     proj_v = v["proj"]
@@ -313,11 +372,26 @@
     lax.fori_loop(second, toks, pair_step, 0, unroll=4)
     extra = bias_v[...] + same[:, None, :] * chain_weight[None, :, :]
 
-    def wait_tok(k, c):
-        tok_copy(k, lax.rem(me + k, n)).wait_recv()
-        return c
-
-    lax.fori_loop(1, n, wait_tok, 0)
+    def pass_line(k, c):
+        arrived(k, seat)
+        to_sibling(k).start()
+        return c
+
+    lax.fori_loop(1, lines, pass_line, 0)
+
+    def pass_across(k, c):
+        arrived(k, across_seat)
+        corner(k).start()
+        return c
+
+    lax.fori_loop(0, lines, pass_across, 0)
+
+    def take(k, c):
+        arrived(k, sibling_seat)
+        arrived(k, corner_seat)
+        return c
+
+    lax.fori_loop(0, lines, take, 0)
     everyone = tok_all[...].reshape(total_tokens, CS)
     keys = dot(everyone, proj_v[:, CS : 2 * CS]).astype(BF16)
     scores = dot_t(expanded, keys) * (1.0 / math.sqrt(HDIM))
@@ -379,10 +453,23 @@
 
     def drain(k, c):
         meta_copy(k, me).wait_send()
-        tok_copy(k, me).wait_send()
         return c
 
     lax.fori_loop(1, n, drain, 0)
+
+    def drain_line(k, c):
+        along_line(k).wait_send()
+        return c
+
+    lax.fori_loop(1, lines, drain_line, 0)
+
+    def drain_rest(k, c):
+        diagonal(k).wait_send()
+        to_sibling(k).wait_send()
+        corner(k).wait_send()
+        return c
+
+    lax.fori_loop(0, lines, drain_rest, 0)
 
     @pl.when(me < n - 1)
     def _():
@@ -468,9 +555,9 @@
             dma((2,)),
         ],
         compiler_params=pltpu.CompilerParams(
-            collective_id=0, has_side_effects=True
+            collective_id=0, has_side_effects=True, vmem_limit_bytes=48 << 20
         ),
-    )(*args)
+    )(*[pltpu.with_memory_space_constraint(x, pltpu.HBM) for x in args])
     return pl.pallas_call(
         hand_over,
         out_shape=shapes,

time: 31.9 us -> 24.5 us (0.77)
  Pallas kernels: 29.5 us -> 23.7 us
  local copies, waits for them, and re-layouts: 1.57 us -> 0 us
    pallas_call x1, Pallas kernels: 28.9 us -> 23.1 us  [shards(): pl.pallas_call(functools.partial(kernel, n), out_shape=shapes, in_specs=[...]
    unnamed x4 -> x0, local copies, waits for them, and re-layouts: 1.57 us -> none
where the time goes in v3:
time: 24.5 us; the launch traced here: 24.4 us
  Pallas kernels  23.7 us (97%)
  between operations  0.65 us (3%)
    pallas_call x1, Pallas kernels, shards(): pl.pallas_call(functools.partial(kernel, n), out_shape=shapes, in_specs=[...  23.1 us
    pallas_call x1, Pallas kernels, shards(): pl.pallas_call(hand_over, out_shape=shapes, in_specs=[vmem, vmem], out_sp...  0.64 us

profile of v3, /device:TPU:5, one launch (start us, length us, event | category | flops | bytes accessed | tf_op | source)
XLA Modules:
  0.0 24.4 jit_solution(15990629612266724370)
XLA Ops:
  0.6 23.1 %shard_map.194 = (bf16[256,128]{1,0:T(8,128)(2,1)S(1)}, bf16[16,768]{1,0:T(8,128)(2,1)S(1)}) custom-call(bf16[256,128]{1,0:T(8,128)(2,1)} %refs_0_.1, s32[1,8]{1,0:T(1,128)} %bitcast.11, s32[1,16]{1,0:T(1,128)} %bitcast.12, s32[1,16]{1,0:T(1,128)} %bitcast.13, s32[1,16]{1,0:T(1,128)} %bitcast.14, bf16[16,768]{1,0:T(8,128)(2,1)} %refs_5_.1, ...), custom_call_target="tpu_custom_call" | custom-call | tf_op jit(solution)/shard_map/pallas_call | solution.py:535
  23.7 0.6 %shard_map.195 = (bf16[256,128]{1,0:T(8,128)(2,1)}, bf16[16,768]{1,0:T(8,128)(2,1)}) custom-call(bf16[256,128]{1,0:T(8,128)(2,1)S(1)} %get-tuple-element.4.atoms_ref, bf16[16,768]{1,0:T(8,128)(2,1)S(1)} %get-tuple-element.5.tokens_ref), custom_call_target="tpu_custom_call" | custom-call | tf_op jit(solution)/shard_map/pallas_call | solution.py:561

commit v4 on v3

--- a/solution.py
+++ b/solution.py
@@ -194,7 +194,7 @@
             at, starts, own_proj[at : at + edge, :CA], own_proj[at - HALO : at + edge + HALO, CA:]
         )
 
-    first, second = 0, toks // 4
+    first, second = 0, 3 * toks // 4
     pl.semaphore_wait(barrier, n - 1)
 
     up = pltpu.make_async_remote_copy(
@@ -343,9 +343,9 @@
         diagonal(k).start()
         return c
 
+    to_sibling(0).start()
+    to_across(0).start()
     lax.fori_loop(1, lines, start_tok, 0)
-    to_across(0).start()
-    to_sibling(0).start()
 
     loads["proj"].wait()
     proj_v = v["proj"]
@@ -356,6 +356,8 @@
     head_mask = ((column_of >= head_row) & (column_of < head_row + HDIM)).astype(F32)
     expanded = (query[:, None, :] * head_mask[None, :, :]).reshape(toks * HEADS, CS).astype(BF16)
 
+    absorbed = dot_t(expanded, proj_v[:, CS : 2 * CS]).astype(BF16)
+
     shift = toks.bit_length() - 1
     token_of = iota((LANES, total_tokens), 1)
     pick = (iota((LANES, total_tokens), 0) == (token_of & (toks - 1))).astype(F32)
@@ -393,8 +395,7 @@
 
     lax.fori_loop(0, lines, take, 0)
     everyone = tok_all[...].reshape(total_tokens, CS)
-    keys = dot(everyone, proj_v[:, CS : 2 * CS]).astype(BF16)
-    scores = dot_t(expanded, keys) * (1.0 / math.sqrt(HDIM))
+    scores = dot_t(absorbed, everyone) * (1.0 / math.sqrt(HDIM))
     scores = scores + extra.reshape(toks * HEADS, total_tokens)
     weights = jnp.exp(scores - jnp.max(scores, axis=-1, keepdims=True))
     denom = jnp.sum(weights, axis=-1, keepdims=True)

time: 24.5 us -> 24.1 us (0.984)
  Pallas kernels: 23.7 us -> 23.3 us
    pallas_call x1, Pallas kernels: 23.1 us -> 22.6 us  [shards(): pl.pallas_call(functools.partial(kernel, n), out_shape=shapes, in_specs=[...]
where the time goes in v4:
time: 24.1 us; the launch traced here: 23.9 us
  Pallas kernels  23.3 us (97%)
  between operations  0.65 us (3%)
    pallas_call x1, Pallas kernels, shards(): pl.pallas_call(functools.partial(kernel, n), out_shape=shapes, in_specs=[...  22.6 us
    pallas_call x1, Pallas kernels, shards(): pl.pallas_call(hand_over, out_shape=shapes, in_specs=[vmem, vmem], out_sp...  0.64 us

profile of v4, /device:TPU:5, one launch (start us, length us, event | category | flops | bytes accessed | tf_op | source)
XLA Modules:
  0.0 23.9 jit_solution(11609991246391634773)
XLA Ops:
  0.6 22.6 %shard_map.194 = (bf16[256,128]{1,0:T(8,128)(2,1)S(1)}, bf16[16,768]{1,0:T(8,128)(2,1)S(1)}) custom-call(bf16[256,128]{1,0:T(8,128)(2,1)} %refs_0_.1, s32[1,8]{1,0:T(1,128)} %bitcast.11, s32[1,16]{1,0:T(1,128)} %bitcast.12, s32[1,16]{1,0:T(1,128)} %bitcast.13, s32[1,16]{1,0:T(1,128)} %bitcast.14, bf16[16,768]{1,0:T(8,128)(2,1)} %refs_5_.1, ...), custom_call_target="tpu_custom_call" | custom-call | tf_op jit(solution)/shard_map/pallas_call | solution.py:536
  23.3 0.6 %shard_map.195 = (bf16[256,128]{1,0:T(8,128)(2,1)}, bf16[16,768]{1,0:T(8,128)(2,1)}) custom-call(bf16[256,128]{1,0:T(8,128)(2,1)S(1)} %get-tuple-element.4.atoms_ref, bf16[16,768]{1,0:T(8,128)(2,1)S(1)} %get-tuple-element.5.tokens_ref), custom_call_target="tpu_custom_call" | custom-call | tf_op jit(solution)/shard_map/pallas_call | solution.py:562
